TPU v7x, 32 devices: a whole 2x2x4 slice. The times are simulated.
32 devices in a mesh: rows: 8 (over z, y), cls: 4 (over x, core).
Axes of the slice: x: 2, y: 2, z: 4, core: 2. Of those that a mesh axis runs over, the one named last changes fastest.
Arguments:
- features: bfloat16 [6144, 2048], P('rows', 'cls'), may hold values from -32 to 32
- prototypes: bfloat16 [2048, 16384], P('rows', 'cls'), may hold values from -1 to 1
Outputs:
- grad_proto: float32 [2048, 16384], P('rows', 'cls')
All inputs are finite; a program needn't handle non-finite values.
Results may differ from a plain program's by a relative error of at most 0.02.
Values may be sent and summed in bfloat16 or wider, within the bound.
A program may use at most 128 MiB of HBM per device.

v0:
```python
import jax
import jax.numpy as jnp
from jax import lax
from jax.sharding import PartitionSpec as P

ITERS = 3
code_temp = 0.2
loss_temp = 0.3


def local(features, prototypes):
    gathered = lax.all_gather(features, "cls", axis=1, tiled=True)
    local_rows = gathered.shape[0]
    local_classes = prototypes.shape[1]
    balance_ratio = float(local_rows * lax.axis_size("rows")) / float(
        local_classes * lax.axis_size("cls")
    )
    columns = gathered
    scores = jnp.dot(
        columns,
        lax.all_gather(prototypes, "rows", axis=0, tiled=True),
        preferred_element_type=jnp.float32,
    )
    local_top = jnp.max(scores, axis=1)
    row_top = lax.pmax(local_top, "cls")
    shifted = scores - row_top[:, None]
    exp_codes = jnp.exp(shifted / code_temp)
    exp_loss = jnp.exp(shifted / loss_temp)
    sink_total, soft_total = lax.psum(
        (jnp.sum(exp_codes, axis=1), jnp.sum(exp_loss, axis=1)), "cls"
    )
    codes = exp_codes / sink_total[:, None]
    for sweep in range(ITERS):
        col_mass = lax.psum(jnp.sum(codes, axis=0), "rows")
        codes = codes * (balance_ratio / col_mass)[None, :]
        row_mass = lax.psum(jnp.sum(codes, axis=1), "cls")
        codes = codes / row_mass[:, None]
    probs_loss = exp_loss / soft_total[:, None]
    slope = ((probs_loss - codes) / loss_temp).astype(jnp.bfloat16)
    columns = gathered
    return lax.psum_scatter(
        lax.dot_general(
            columns, slope, (((0,), (0,)), ((), ())), preferred_element_type=jnp.float32
        ).astype(jnp.bfloat16),
        "rows",
        scatter_dimension=0,
        tiled=True,
    ).astype(jnp.float32)


def solution(mesh):
    return jax.shard_map(
        local,
        mesh=mesh,
        in_specs=(P("rows", "cls"), P("rows", "cls")),
        out_specs=P("rows", "cls"),
        check_vma=False,
    )
```

profile of v0, /device:TPU:0, one launch (start us, length us, event | category | flops | bytes accessed | tf_op | source)
XLA Modules:
  0.0 786.4 jit_solution(6704144554605490783)
XLA Ops:
  6.5 0.7 all-gather.3.cloned.1.call-update
  7.3 0.7 all-gather.5.cloned.1.call-update
  8.0 0.0 reduce-scatter.2.cloned.1.call-start
  8.1 32.1 %all-gather.3.cloned.1.call-done = bf16[768,2048]{1,0:T(8,128)(2,1)} async-done(((bf16[768,512]{1,0:T(8,128)(2,1)}), bf16[768,2048]{1,0:T(8,128)(2,1)}) %all-gather.3.cloned.1.call-update) | async-done | bytes 3145744 | tf_op jit(solution)/shard_map/all_gather | solution.py:12
  40.2 229.8 %all-gather.5.cloned.1.call-done = bf16[2048,4096]{1,0:T(8,128)(2,1)} async-done(((bf16[256,4096]{1,0:T(8,128)(2,1)}), bf16[2048,4096]{1,0:T(8,128)(2,1)}) %all-gather.5.cloned.1.call-update) | async-done | bytes 16777232 | tf_op jit(solution)/shard_map/all_gather | solution.py:21
  270.0 20.3 %fusion.8 = (f32[768]{0:T(1024)S(1)}, f32[768,4096]{1,0:T(8,128)}) fusion(bf16[768,2048]{1,0:T(8,128)(2,1)} %all-gather.3.cloned.1.call-done, bf16[2048,4096]{1,0:T(8,128)(2,1)} %all-gather.5.cloned.1.call-done), kind=kOutput, calls=%fused_computation.19 | convolution fusion | flops 12888046592 | bytes 32508928 | tf_op jit(solution)/shard_map/dot_general | solution.py:19
  290.3 6.1 pmax.7
  296.4 7.1 fusion
  303.5 6.1 psum.57
  309.7 11.3 %fusion.6 = (f32[4096]{0:T(1024)S(1)}, f32[768,4096]{1,0:T(8,128)}) fusion(f32[768]{0:T(1024)S(1)} %psum.57, f32[768,4096]{1,0:T(8,128)} %get-tuple-element.14, f32[768]{0:T(1024)S(1)} %pmax.7), kind=kLoop, calls=%fused_computation.18 | loop fusion | flops 12578816 | bytes 25188352 | tf_op jit(solution)/shard_map/reduce_sum | solution.py:34
  320.9 34.6 %psum.58 = f32[4096]{0:T(1024)S(1)} all-reduce(f32[4096]{0:T(1024)S(1)} %get-tuple-element.11), channel_id=1, replica_groups=mesh['rows'=8,'cls'=4] {'rows'}, use_global_device_ids=true, to_apply=%region_7.0 | all-reduce | flops 4096 | bytes 32768 | tf_op jit(solution)/shard_map/psum | solution.py:34
  355.6 5.5 multiply_reduce_fusion.2
  361.1 5.8 psum.59
  366.8 6.4 fusion.4
  373.3 33.2 %psum.60 = f32[4096]{0:T(1024)S(1)} all-reduce(f32[4096]{0:T(1024)S(1)} %fusion.4), channel_id=1, replica_groups=mesh['rows'=8,'cls'=4] {'rows'}, use_global_device_ids=true, to_apply=%region_11.0 | all-reduce | flops 4096 | bytes 32768 | tf_op jit(solution)/shard_map/psum | solution.py:34
  406.5 6.0 multiply_reduce_fusion.1
  412.4 5.8 psum.61
  418.2 11.3 %fusion.5 = (f32[4096]{0:T(1024)S(1)}, f32[768,4096]{1,0:T(8,128)}) fusion(f32[768]{0:T(1024)S(1)} %psum.61, f32[4096]{0:T(1024)S(1)} %broadcast_divide_fusion.1, f32[768]{0:T(1024)S(1)} %psum.59, f32[768,4096]{1,0:T(8,128)} %get-tuple-element.12, f32[4096]{0:T(1024)S(1)} %broadcast_divide_fusion.2), kind=kLoop, calls=%fused_computation.17 | loop fusion | flops 15724544 | bytes 25221120 | tf_op jit(solution)/shard_map/reduce_sum | solution.py:34
  429.5 33.2 %psum.62 = f32[4096]{0:T(1024)S(1)} all-reduce(f32[4096]{0:T(1024)S(1)} %get-tuple-element.9), channel_id=1, replica_groups=mesh['rows'=8,'cls'=4] {'rows'}, use_global_device_ids=true, to_apply=%region_15.0 | all-reduce | flops 4096 | bytes 32768 | tf_op jit(solution)/shard_map/psum | solution.py:34
  462.7 5.5 multiply_reduce_fusion
  468.2 5.9 all-reduce
  474.1 22.6 %convert_bitcast_fusion = bf16[2048,4096]{0,1:T(8,128)(2,1)} fusion(bf16[768,2048]{1,0:T(8,128)(2,1)S(1)} %copy-done, f32[768,4096]{1,0:T(8,128)} %get-tuple-element.10, f32[768,4096]{1,0:T(8,128)} %get-tuple-element.14, f32[768]{0:T(1024)S(1)} %get-tuple-element.7, f32[4096]{0:T(1024)S(1)} %broadcast_divide_fusion, f32[768]{0:T(1024)S(1)} %get-tuple-element.8, ...), kind=kOutput, calls=%fused_computation | convolution fusion | flops 12918456320 | bytes 45114368 | tf_op jit(solution)/shard_map/dot_general | solution.py:42
  496.8 278.8 %reduce-scatter.2.cloned.1.call-done = bf16[256,4096]{0,1:T(8,128)(2,1)} async-done(((bf16[2048,4096]{0,1:T(8,128)(2,1)}), bf16[256,4096]{0,1:T(8,128)(2,1)}) %reduce-scatter.2.cloned.1.call-update) | async-done | bytes 2097168 | tf_op jit(solution)/shard_map/reduce_scatter | solution.py:41
  775.6 4.3 copy.3
  (8 shorter events, 0.1 us)
Async XLA Ops:
  6.5 33.6 %all-gather.3.cloned.1.call-start = ((), (), s32[]{:S(2)}) async-start(), calls=%async_computation.1 | async-start | bytes 3932160 | tf_op jit(solution)/shard_map/all_gather | solution.py:12
  7.3 262.7 %all-gather.5.cloned.1.call-start = ((), (), s32[]{:S(2)}) async-start(), calls=%async_computation.2 | async-start | bytes 18874368 | tf_op jit(solution)/shard_map/all_gather | solution.py:21
  8.0 767.6 %reduce-scatter.2.cloned.1.call-start = ((), (), s32[]{:S(2)}) async-start(), calls=%async_computation.3 | async-start | bytes 18874368 | tf_op jit(solution)/shard_map/reduce_scatter | solution.py:41
  429.5 44.6 %copy-start = (bf16[768,2048]{1,0:T(8,128)(2,1)S(1)}, bf16[768,2048]{1,0:T(8,128)(2,1)}, u32[]{:S(2)}) copy-start(bf16[768,2048]{1,0:T(8,128)(2,1)} %all-gather.3.cloned.1.call-done) | copy-start | bytes 9437188
Sparse Core Ops, SparseCore 0:
  8.9 31.2 all-gather.2
  42.3 227.6 all-gather.4
  496.9 278.6 reduce-scatter.1
where the time goes:
time: 787 us; the launch traced here: 786 us
  waiting for transfers between devices  542 us (69%)
  blocking collectives  131 us (17%)
  other arithmetic  53.1 us (7%)
  matrix products  42.9 us (5%)
  between operations  13.1 us (2%)
    reduce_scatter x1, waiting for transfers between devices, local(): lax.psum_scatter(lax.dot_general(columns, slope, (((0,), (0,)), ((), ()))...  279 us
    all_gather x1, waiting for transfers between devices, local(): lax.all_gather(prototypes, 'rows', axis=0, tiled=True)  230 us
    psum x3, blocking collectives, local(): col_mass = lax.psum(jnp.sum(codes, axis=0), 'rows')  101 us
    all_gather x1, waiting for transfers between devices, local(): gathered = lax.all_gather(features, 'cls', axis=1, tiled=True)  32.1 us
    reduce_sum x3, other arithmetic, local(): col_mass = lax.psum(jnp.sum(codes, axis=0), 'rows')  29 us
    dot_general x1, matrix products, local(): lax.dot_general(columns, slope, (((0,), (0,)), ((), ())), preferred_eleme...  22.6 us
    dot_general x1, matrix products, local(): jnp.dot(columns, lax.all_gather(prototypes, 'rows', axis=0, tiled=True),...  20.3 us
    psum x3, blocking collectives, local(): row_mass = lax.psum(jnp.sum(codes, axis=1), 'cls')  17.4 us
  transfers between devices with their start and end apart: 3, of which 3 were waited for; matrix products, arithmetic and copies ran while one was open for 0% of the time, Pallas kernels for 0%

commit v1 on v0

--- a/solution.py
+++ b/solution.py
@@ -9,7 +9,17 @@
 
 
 def local(features, prototypes):
-    gathered = lax.all_gather(features, "cls", axis=1, tiled=True)
+    count, index, rows = (lax.axis_size("cls"), lax.axis_index("cls"), features.shape[1])
+    right = [(i, (i + 1) % count) for i in range(count)]
+    gathered = jnp.zeros(
+        (*features.shape[:1], count * rows, *features.shape[1 + 1 :]), features.dtype
+    )
+    held = features
+    for step in range(count):
+        owner = (index - step) % count
+        gathered = lax.dynamic_update_slice_in_dim(gathered, held, owner * rows, axis=1)
+        if step < count - 1:
+            held = lax.ppermute(held, "cls", right)
     local_rows = gathered.shape[0]
     local_classes = prototypes.shape[1]
     balance_ratio = float(local_rows * lax.axis_size("rows")) / float(

time: 787 us -> 760 us (0.966)
  waiting for transfers between devices: 542 us -> 504 us
    all_gather x1, waiting for transfers between devices: 230 us -> 195 us  [local(): lax.all_gather(prototypes, 'rows', axis=0, tiled=True)]
    all_gather x1 -> x0, waiting for transfers between devices: 32.1 us -> none  [local(): gathered = lax.all_gather(features, 'cls', axis=1, tiled=True)]
    ppermute x0 -> x3, waiting for transfers between devices: none -> 30.9 us  [local(): held = lax.ppermute(held, 'cls', right)]
  transfers between devices with their start and end apart: 3 -> 5, of which waited for: 3 -> 5; matrix products, arithmetic and copies ran while one was open for 0% -> 1% of each run, Pallas kernels for 0% -> 0%
where the time goes in v1:
time: 760 us; the launch traced here: 759 us
  waiting for transfers between devices  504 us (66%)
  blocking collectives  130 us (17%)
  other arithmetic  57.2 us (8%)
  matrix products  46.8 us (6%)
  between operations  13.5 us (2%)
    reduce_scatter x1, waiting for transfers between devices, local(): lax.psum_scatter(lax.dot_general(columns, slope, (((0,), (0,)), ((), ()))...  278 us
    all_gather x1, waiting for transfers between devices, local(): lax.all_gather(prototypes, 'rows', axis=0, tiled=True)  195 us
    psum x3, blocking collectives, local(): col_mass = lax.psum(jnp.sum(codes, axis=0), 'rows')  101 us
    ppermute x3, waiting for transfers between devices, local(): held = lax.ppermute(held, 'cls', right)  30.9 us
    reduce_sum x3, other arithmetic, local(): col_mass = lax.psum(jnp.sum(codes, axis=0), 'rows')  29 us
    dot_general x1, matrix products, local(): lax.dot_general(columns, slope, (((0,), (0,)), ((), ())), preferred_eleme...  27.4 us
    dot_general x1, matrix products, local(): jnp.dot(columns, lax.all_gather(prototypes, 'rows', axis=0, tiled=True),...  19.4 us
    psum x3, blocking collectives, local(): row_mass = lax.psum(jnp.sum(codes, axis=1), 'cls')  17.4 us
  transfers between devices with their start and end apart: 5, of which 5 were waited for; matrix products, arithmetic and copies ran while one was open for 1% of the time, Pallas kernels for 0%

profile of v1, /device:TPU:0, one launch (start us, length us, event | category | flops | bytes accessed | tf_op | source)
XLA Modules:
  0.0 759.2 jit_solution(4585161158435188429)
XLA Ops:
  7.8 11.8 %collective-permute-done = bf16[768,512]{1,0:T(8,128)(2,1)S(1)} collective-permute-done((bf16[768,512]{1,0:T(8,128)(2,1)}, bf16[768,512]{1,0:T(8,128)(2,1)S(1)}, u32[]{:S(2)}, u32[]{:S(2)}) %collective-permute-start) | collective-permute-done | bytes 786464 | tf_op jit(solution)/shard_map/ppermute | solution.py:22
  20.5 11.5 %collective-permute-done.1 = bf16[768,512]{1,0:T(8,128)(2,1)} collective-permute-done((bf16[768,512]{1,0:T(8,128)(2,1)S(1)}, bf16[768,512]{1,0:T(8,128)(2,1)}, u32[]{:S(2)}, u32[]{:S(2)}) %collective-permute-start.1) | collective-permute-done | bytes 786464 | tf_op jit(solution)/shard_map/ppermute | solution.py:22
  33.7 1.3 constant_dynamic-update-slice_fusion.2
  36.2 7.6 collective-permute-done.2
  45.0 194.8 %all-gather.2.cloned.1.call-done = bf16[2048,4096]{1,0:T(8,128)(2,1)} async-done(((bf16[256,4096]{1,0:T(8,128)(2,1)}), bf16[2048,4096]{1,0:T(8,128)(2,1)}) %all-gather.2.cloned.1.call-update) | async-done | bytes 16777232 | tf_op jit(solution)/shard_map/all_gather | solution.py:31
  239.8 19.4 %fusion.8 = (f32[768]{0:T(1024)S(1)}, f32[768,4096]{1,0:T(8,128)}) fusion(bf16[768,2048]{1,0:T(8,128)(2,1)S(1)} %constant_dynamic-update-slice_fusion, bf16[2048,4096]{1,0:T(8,128)(2,1)} %all-gather.2.cloned.1.call-done), kind=kOutput, calls=%fused_computation.23 | convolution fusion | flops 12888046592 | bytes 32508928 | tf_op jit(solution)/shard_map/dot_general | solution.py:29
  259.2 6.1 pmax.7
  265.4 7.1 fusion
  272.5 6.1 psum.57
  278.6 11.3 %fusion.6 = (f32[4096]{0:T(1024)S(1)}, f32[768,4096]{1,0:T(8,128)}) fusion(f32[768]{0:T(1024)S(1)} %psum.57, f32[768,4096]{1,0:T(8,128)} %get-tuple-element.14, f32[768]{0:T(1024)S(1)} %pmax.7), kind=kLoop, calls=%fused_computation.22 | loop fusion | flops 12578816 | bytes 25188352 | tf_op jit(solution)/shard_map/reduce_sum | solution.py:44
  289.9 34.6 %psum.58 = f32[4096]{0:T(1024)S(1)} all-reduce(f32[4096]{0:T(1024)S(1)} %get-tuple-element.11), channel_id=1, replica_groups=mesh['rows'=8,'cls'=4] {'rows'}, use_global_device_ids=true, to_apply=%region_7.8 | all-reduce | flops 4096 | bytes 32768 | tf_op jit(solution)/shard_map/psum | solution.py:44
  324.6 5.5 multiply_reduce_fusion.2
  330.0 5.8 psum.59
  335.8 6.4 fusion.4
  342.3 33.2 %psum.60 = f32[4096]{0:T(1024)S(1)} all-reduce(f32[4096]{0:T(1024)S(1)} %fusion.4), channel_id=1, replica_groups=mesh['rows'=8,'cls'=4] {'rows'}, use_global_device_ids=true, to_apply=%region_11.12 | all-reduce | flops 4096 | bytes 32768 | tf_op jit(solution)/shard_map/psum | solution.py:44
  375.4 6.0 multiply_reduce_fusion.1
  381.4 5.8 psum.61
  387.2 11.3 %fusion.5 = (f32[4096]{0:T(1024)S(1)}, f32[768,4096]{1,0:T(8,128)}) fusion(f32[768]{0:T(1024)S(1)} %psum.61, f32[4096]{0:T(1024)S(1)} %broadcast_divide_fusion.1, f32[768]{0:T(1024)S(1)} %psum.59, f32[768,4096]{1,0:T(8,128)} %get-tuple-element.12, f32[4096]{0:T(1024)S(1)} %broadcast_divide_fusion.2), kind=kLoop, calls=%fused_computation.21 | loop fusion | flops 15724544 | bytes 25221120 | tf_op jit(solution)/shard_map/reduce_sum | solution.py:44
  398.5 33.0 %psum.62 = f32[4096]{0:T(1024)S(1)} all-reduce(f32[4096]{0:T(1024)S(1)} %get-tuple-element.9), channel_id=1, replica_groups=mesh['rows'=8,'cls'=4] {'rows'}, use_global_device_ids=true, to_apply=%region_15.16 | all-reduce | flops 4096 | bytes 32768 | tf_op jit(solution)/shard_map/psum | solution.py:44
  431.4 5.5 multiply_reduce_fusion
  436.9 5.9 all-reduce
  442.8 27.4 %convolution_convert_fusion = bf16[2048,4096]{1,0:T(8,128)(2,1)} fusion(bf16[768,2048]{1,0:T(8,128)(2,1)S(1)} %constant_dynamic-update-slice_fusion, f32[768,4096]{1,0:T(8,128)} %get-tuple-element.10, f32[768,4096]{1,0:T(8,128)} %get-tuple-element.14, f32[768]{0:T(1024)S(1)} %get-tuple-element.7, f32[4096]{0:T(1024)S(1)} %broadcast_divide_fusion, ...), kind=kOutput, calls=%fused_computation | convolution fusion | flops 12918456320 | bytes 45114368 | tf_op jit(solution)/shard_map/dot_general | solution.py:52
  470.2 278.0 %reduce-scatter.2.cloned.1.call-done = bf16[256,4096]{1,0:T(8,128)(2,1)} async-done(((bf16[2048,4096]{1,0:T(8,128)(2,1)}), bf16[256,4096]{1,0:T(8,128)(2,1)}) %reduce-scatter.2.cloned.1.call-update) | async-done | bytes 2097168 | tf_op jit(solution)/shard_map/reduce_scatter | solution.py:51
  748.2 4.1 convert_element_type.11
  (16 shorter events, 6.3 us)
Async XLA Ops:
  6.5 233.3 %all-gather.2.cloned.1.call-start = ((), (), s32[]{:S(2)}) async-start(), calls=%async_computation.1 | async-start | bytes 18874368 | tf_op jit(solution)/shard_map/all_gather | solution.py:31
  7.3 741.0 %reduce-scatter.2.cloned.1.call-start = ((), (), s32[]{:S(2)}) async-start(), calls=%async_computation.2 | async-start | bytes 18874368 | tf_op jit(solution)/shard_map/reduce_scatter | solution.py:51
  7.3 12.3 %collective-permute-start = (bf16[768,512]{1,0:T(8,128)(2,1)}, bf16[768,512]{1,0:T(8,128)(2,1)S(1)}, u32[]{:S(2)}, u32[]{:S(2)}) collective-permute-start(bf16[768,512]{1,0:T(8,128)(2,1)} %param.2), channel_id=1, source_target_pairs={{0,1},{1,2},{2,3},{3,0},{4,5},{5,6},{6,7},{7,4},{8,9},{9,10},{10,1... | collective-permute-start | bytes 2359304 | tf_op jit(solution)/shard_map/ppermute | solution.py:22
  19.6 0.9 copy-start
  20.5 11.5 %collective-permute-start.1 = (bf16[768,512]{1,0:T(8,128)(2,1)S(1)}, bf16[768,512]{1,0:T(8,128)(2,1)}, u32[]{:S(2)}, u32[]{:S(2)}) collective-permute-start(bf16[768,512]{1,0:T(8,128)(2,1)S(1)} %collective-permute-done), channel_id=1, source_target_pairs={{0,1},{1,2},{2,3},{3,0},{4,5},{5,6},{6,7},{7,4},{8,9},{9,10},{10,1... | collective-permute-start | bytes 2359304 | tf_op jit(solution)/shard_map/ppermute | solution.py:22
  32.0 11.7 %collective-permute-start.2 = (bf16[768,512]{1,0:T(8,128)(2,1)}, bf16[768,512]{1,0:T(8,128)(2,1)}, u32[]{:S(2)}, u32[]{:S(2)}) collective-permute-start(bf16[768,512]{1,0:T(8,128)(2,1)} %collective-permute-done.1), channel_id=1, source_target_pairs={{0,1},{1,2},{2,3},{3,0},{4,5},{5,6},{6,7},{7,4},{8,9},{9,10},{10,1... | collective-permute-start | bytes 2359304 | tf_op jit(solution)/shard_map/ppermute | solution.py:22
Sparse Core Ops, SparseCore 0:
  9.5 230.3 all-gather.1
  470.3 277.8 reduce-scatter.1
